TPU v7x, 32 devices: a whole 2x2x4 slice. The times are simulated.
32 devices in a mesh: section: 4 (over z), tile: 8 (over y, x, core).
Axes of the slice: x: 2, y: 2, z: 4, core: 2. Of those that a mesh axis runs over, the one named last changes fastest.
Arguments:
- raw_echo: bfloat16 [2, 2048, 8192], P(None, 'tile', 'section'), may hold values from -6 to 6
- footprint: int32 [4, 8, 8], P('section', 'tile'), may hold values from 0 to 255, as said below
- window_start: int32 [4, 256], P('section', 'tile'), may hold values from 0 to 2047
Outputs:
- image: bfloat16 [4, 8, 1024, 2048], P('section', 'tile')
Inputs may be any that keep to these rules, and one draw needn't show every extreme that they name: `footprint`: each list names 8 different pulse blocks; at most 2 of them lie among the 32 blocks k * 32 to (k + 1) * 32 - 1 of one index k of tile, and in every list some index supplies exactly 2.
All inputs are finite; a program needn't handle non-finite values.
Results may differ from a plain program's by a relative error of at most 0.0071.
Values may be sent and summed in bfloat16 or wider, within the bound.
No kernel may reach another device: no remote copies, remote signals or barrier semaphores. Data moves between devices by JAX's collectives and lax.ppermute only.
A program may use at most 128 MiB of HBM per device.

v0:
```python
import math
import jax
import jax.numpy as jnp
from jax import lax
from jax.sharding import PartitionSpec as P

KC = 128
WIN = 256
PR = 1024
PC = 1024
NP = 8


def passed_along(value, axis, by):
    devices = lax.axis_size(axis)
    pairs = [(i, i + by) for i in range(devices) if 0 <= i + by < devices]
    return lax.ppermute(value, axis, pairs)


def chirp_table(length):
    row_index = lax.broadcasted_iota(jnp.int32, (2 * length, length), 0)
    col_index = lax.broadcasted_iota(jnp.int32, (2 * length, length), 1)
    lag_count = row_index - col_index
    inside = (lag_count >= 0) & (lag_count < length)
    lag_safe = jnp.where(inside, lag_count, 0)
    turn_count = (lag_safe * lag_safe % (2 * length)).astype(jnp.float32)
    phase_angle = turn_count * jnp.float32(math.pi / length)
    scaling = jnp.float32(1.0 / math.sqrt(length))
    real_part = jnp.where(inside, jnp.cos(phase_angle) * scaling, jnp.float32(0.0))
    imag_part = jnp.where(inside, jnp.sin(phase_angle) * scaling, jnp.float32(0.0))
    return (real_part.astype(jnp.bfloat16), imag_part.astype(jnp.bfloat16))


def compress(raw_part, length, keep):
    real_tab, imag_tab = chirp_table(length)
    pulses = raw_part.shape[1]
    blocks = keep // length
    pieces = raw_part.reshape(2, pulses, blocks + 1, length)
    paired = jnp.concatenate([pieces[:, :, :-1], pieces[:, :, 1:]], axis=3).reshape(
        2, pulses * blocks, 2 * length
    )
    real_in = paired[0]
    imag_in = paired[1]
    out_real = jnp.dot(real_in, real_tab, preferred_element_type=jnp.float32) + jnp.dot(
        imag_in, imag_tab, preferred_element_type=jnp.float32
    )
    out_imag = jnp.dot(imag_in, real_tab, preferred_element_type=jnp.float32) - jnp.dot(
        real_in, imag_tab, preferred_element_type=jnp.float32
    )
    stacked = jnp.stack([out_real, out_imag]).reshape(2, pulses, keep)
    return stacked.astype(jnp.bfloat16)


def interp_table(pixel_rows, window_bins):
    upsample = pixel_rows // window_bins
    row_index = lax.broadcasted_iota(jnp.float32, (pixel_rows, window_bins), 0)
    bin_index = lax.broadcasted_iota(jnp.float32, (pixel_rows, window_bins), 1)
    centre = (row_index + 0.5) / upsample - 0.5
    offset = bin_index - centre
    tapering = jnp.cos(offset * (math.pi / 8.0)) ** 2
    kernel = jnp.where(jnp.abs(offset) < 4.0, jnp.sinc(offset) * tapering, 0.0)
    return kernel.astype(jnp.bfloat16)


def tile_image(chosen, block_ids, row_pos, col_pos, interp, pixel_cols):
    entries = chosen.shape[0]
    per_block = chosen.shape[1]
    window_bins = chosen.shape[3]
    merged = chosen.reshape(entries * per_block, 2 * window_bins)
    pulse_ids = (
        block_ids[:, None] * per_block + jnp.arange(per_block, dtype=jnp.int32)[None, :]
    ).reshape(-1)
    columns = col_pos * pixel_cols + jnp.arange(pixel_cols, dtype=jnp.int32) + 1 + 7 * row_pos
    scrambled = columns * 40503 % 65521
    residue = pulse_ids[:, None] * scrambled[None, :] % 65521
    phase_angle = residue.astype(jnp.float32) * jnp.float32(2.0 * math.pi / 65521.0)
    steer_real = jnp.cos(phase_angle).astype(jnp.bfloat16)
    steer_imag = jnp.sin(phase_angle).astype(jnp.bfloat16)
    contract = (((0,), (0,)), ((), ()))
    with_real = lax.dot_general(merged, steer_real, contract, preferred_element_type=jnp.float32)
    with_imag = lax.dot_general(merged, steer_imag, contract, preferred_element_type=jnp.float32)
    scaling = jnp.float32(1.0 / math.sqrt(entries * per_block))
    focus_real = (with_real[:window_bins] - with_imag[window_bins:]) * scaling
    focus_imag = (with_imag[:window_bins] + with_real[window_bins:]) * scaling
    focused = jnp.concatenate([focus_real, focus_imag], axis=1).astype(jnp.bfloat16)
    return jnp.dot(interp, focused, preferred_element_type=jnp.float32).astype(jnp.bfloat16)


def cut_windows(extended, starts, per_block):
    pulses = extended.shape[1]
    span_bins = extended.shape[2]
    grouped = jnp.transpose(
        extended.reshape(2, pulses // per_block, per_block, span_bins), (1, 2, 0, 3)
    )

    def one_block(block_data, start):
        return lax.dynamic_slice_in_dim(block_data, start, WIN, 2)

    return jax.vmap(one_block)(grouped, starts)


def local(raw_echo, footprint, window_start):
    bin_count = raw_echo.shape[2]
    next_rim = passed_along(raw_echo[:, :, :KC], "section", -1)
    own_part = compress(jnp.concatenate([raw_echo, next_rim], axis=2), KC, bin_count)
    next_bins = passed_along(own_part[:, :, :WIN], "section", -1)
    extended = jnp.concatenate([own_part, next_bins], axis=2)
    windows = cut_windows(extended, window_start[0], NP)
    my_list = footprint[0, 0]
    tile_pos = lax.axis_index("tile")
    row_pos = lax.axis_index("section")
    all_blocks = lax.all_gather(windows, "tile", axis=0, tiled=True)
    chosen = jnp.take(all_blocks, my_list, axis=0)
    interp = interp_table(PR, WIN)
    image = tile_image(chosen, my_list, row_pos, tile_pos, interp, PC)
    return image[None, None]


def solution(mesh):
    in_specs = (P(None, "tile", "section"), P("section", "tile", None), P("section", "tile"))
    out_specs = P("section", "tile", None, None)
    return jax.shard_map(local, mesh=mesh, in_specs=in_specs, out_specs=out_specs, check_vma=False)
```

profile of v0, /device:TPU:0, one launch (start us, length us, event | category | flops | bytes accessed | tf_op | source)
XLA Modules:
  0.0 181.1 jit_solution(12100500757804425028)
XLA Ops:
  6.5 2.8 %copy.15 = bf16[2,256,2048]{1,2,0:T(8,128)(2,1)S(1)} copy(bf16[2,256,2048]{2,1,0:T(8,128)(2,1)} %param.3) | data formatting | bytes 4194304 | tf_op args[0]
  9.4 1.3 collective-permute-start
  10.7 7.1 %collective-permute-done = bf16[2,256,128]{1,2,0:T(8,128)(2,1)S(1)} collective-permute-done((bf16[2,256,128]{1,2,0:T(8,128)(2,1)S(1)}, bf16[2,256,128]{1,2,0:T(8,128)(2,1)S(1)}, u32[]{:S(2)}, u32[]{:S(2)}) %collective-permute-start) | collective-permute-done | bytes 131104 | tf_op jit(solution)/shard_map/ppermute | solution.py:17
  17.8 0.1 pad_maximum_fusion
  18.0 0.5 fusion.123
  18.5 2.3 %pad_maximum_fusion.1 = (bf16[1,256,16,256]{1,3,2,0:T(8,128)(2,1)}, bf16[1,256,16,256]{1,3,2,0:T(8,128)(2,1)}) fusion(bf16[2,256,16,128]{1,3,2,0:T(8,128)(2,1)S(1)} %get-tuple-element.9, bf16[2,256,16,128]{1,3,2,0:T(8,128)(2,1)S(1)} %get-tuple-element.10), kind=kLoop, calls=%fused_computation.12 | loop fusion | flops 8388608 | bytes 8388608 | tf_op jit(solution)/shard_map/concatenate | solution.py:39
  20.8 3.3 %copy.17 = bf16[1,256,16,256]{3,2,1,0:T(8,128)(2,1)S(1)} copy(bf16[1,256,16,256]{1,3,2,0:T(8,128)(2,1)} %get-tuple-element.7) | data formatting | bytes 4194304 | tf_op jit(solution)/shard_map/slice | solution.py:43
  24.1 2.5 %fusion.63 = f32[4096,128]{1,0:T(8,128)} fusion(bf16[4096,256]{1,0:T(8,128)(2,1)S(1)} %bitcast.27), kind=kOutput, calls=%fused_computation.95 | convolution fusion | flops 269156352 | bytes 4194304 | tf_op jit(solution)/shard_map/dot_general | solution.py:47
  26.6 4.5 %copy.16 = bf16[1,256,16,256]{3,2,1,0:T(8,128)(2,1)} copy(bf16[1,256,16,256]{1,3,2,0:T(8,128)(2,1)} %get-tuple-element.8) | data formatting | bytes 4194304 | tf_op jit(solution)/shard_map/slice | solution.py:42
  31.1 4.2 %fusion.64 = f32[4096,128]{1,0:T(8,128)} fusion(bf16[4096,256]{1,0:T(8,128)(2,1)} %bitcast.29), kind=kOutput, calls=%fused_computation.96 | convolution fusion | flops 269156352 | bytes 4194304 | tf_op jit(solution)/shard_map/dot_general | solution.py:44
  35.4 1.2 fusion.1
  36.6 1.3 stack.10
  37.9 2.8 %fusion = bf16[4096,128]{1,0:T(8,128)(2,1)S(1)} fusion(f32[4096,128]{1,0:T(8,128)} %fusion.64, bf16[4096,256]{1,0:T(8,128)(2,1)S(1)} %bitcast.28), kind=kOutput, calls=%fused_computation.4 | convolution fusion | flops 270204928 | bytes 5242880 | tf_op jit(solution)/shard_map/dot_general | solution.py:44
  40.7 0.5 stack.9
  41.2 0.1 constant_dynamic-update-slice_fusion.1
  41.3 0.6 copy-done.2
  42.0 1.5 collective-permute-start.1
  43.5 7.9 %collective-permute-done.1 = bf16[2,256,256]{2,1,0:T(8,128)(2,1)S(1)} collective-permute-done((bf16[2,256,256]{2,1,0:T(8,128)(2,1)S(1)}, bf16[2,256,256]{2,1,0:T(8,128)(2,1)S(1)}, u32[]{:S(2)}, u32[]{:S(2)}) %collective-permute-start.1) | collective-permute-done | bytes 262176 | tf_op jit(solution)/shard_map/ppermute | solution.py:17
  51.4 0.2 maximum_bitcast_fusion
  51.6 60.6 %copy.18 = bf16[2,32,8,2304]{2,0,1,3:T(2,128)(2,1)} copy(bf16[2,32,8,2304]{3,2,1,0:T(8,128)(2,1)S(1)} %maximum_bitcast_fusion) | data formatting | bytes 4718592 | tf_op jit(solution)/shard_map/reshape | solution.py:93
  112.2 11.5 %gather_fusion.1 = bf16[32,8,2,256]{1,2,3,0:T(2,128)(2,1)} fusion(bf16[32,8,2,2304]{1,2,0,3:T(2,128)(2,1)} %bitcast.26, s32[32]{0:T(128)S(1)} %fusion.72), kind=kCustom, calls=%fused_computation.1 | custom fusion | bytes 524800 | tf_op jit(solution)/shard_map/vmap()/gather | solution.py:97
  123.8 9.2 %copy.19 = bf16[32,8,2,256]{3,1,2,0:T(8,128)(2,1)} copy(bf16[32,8,2,256]{1,2,3,0:T(2,128)(2,1)} %gather_fusion.1) | data formatting | bytes 524288 | tf_op jit(solution)/shard_map/vmap()/gather | solution.py:97
  133.0 0.1 iota_add_fusion
  133.1 0.1 add.195
  133.2 0.1 broadcast_in_dim.34
  133.3 0.1 broadcast_in_dim.35
  133.4 27.7 %all-gather.2.cloned.1.call-done = bf16[256,8,2,256]{3,1,2,0:T(8,128)(2,1)} async-done(((bf16[32,8,2,256]{3,1,2,0:T(8,128)(2,1)}), bf16[256,8,2,256]{3,1,2,0:T(8,128)(2,1)}) %all-gather.2.cloned.1.call-update) | async-done | bytes 2097168 | tf_op jit(solution)/shard_map/all_gather | solution.py:112
  161.1 2.1 %gather_fusion = bf16[8,8,2,256]{3,1,2,0:T(8,128)(2,1)S(1)} fusion(bf16[256,8,2,256]{3,1,2,0:T(8,128)(2,1)} %all-gather.2.cloned.1.call-done, s32[1024]{0:T(1024)S(1)} %pad_clamp_fusion), kind=kCustom, calls=%fused_computation | custom fusion | bytes 131104 | tf_op jit(solution)/shard_map/jit(_take)/gather | solution.py:113
  163.3 1.4 fusion.48
  164.7 1.4 fusion.49
  166.1 0.5 fusion.14
  166.6 7.6 %convert_bitcast_fusion = bf16[1,1,1024,2048]{3,2,1,0:T(8,128)(2,1)} fusion(bf16[256,1024]{1,0:T(8,128)(2,1)S(1)} %get-tuple-element.6, bf16[256,1024]{1,0:T(8,128)(2,1)S(1)} %get-tuple-element.5, f32[1024]{0:T(1024)S(1)} %multiply_add_fusion.1), kind=kOutput, calls=%fused_computation.8 | convolution fusion | flops 1088421888 | bytes 5246976 | tf_op jit(solution)/shard_map/dot_general | solution.py:86
  (21 shorter events, 0.2 us)
Async XLA Ops:
  6.5 154.6 %all-gather.2.cloned.1.call-start = ((), (), s32[]{:S(2)}) async-start(), calls=%async_computation | async-start | bytes 2359296 | tf_op jit(solution)/shard_map/all_gather | solution.py:112
  9.4 8.4 %collective-permute-start = (bf16[2,256,128]{1,2,0:T(8,128)(2,1)S(1)}, bf16[2,256,128]{1,2,0:T(8,128)(2,1)S(1)}, u32[]{:S(2)}, u32[]{:S(2)}) collective-permute-start(bf16[2,256,128]{1,2,0:T(8,128)(2,1)S(1)} %slice.51), channel_id=1, source_target_pairs={{8,0},{16,8},{24,16},{9,1},{17,9},{25,17},{10,2},{18,10},{26,18},{... | collective-permute-start | bytes 393224 | tf_op jit(solution)/shard_map/ppermute | solution.py:17
  31.1 4.3 %copy-start = (bf16[1,256,16,256]{3,2,1,0:T(8,128)(2,1)S(1)}, bf16[1,256,16,256]{3,2,1,0:T(8,128)(2,1)}, u32[]{:S(2)}) copy-start(bf16[1,256,16,256]{3,2,1,0:T(8,128)(2,1)} %copy.16) | copy-start | bytes 6291460
  31.1 4.3 %copy-start.1 = (f32[4096,128]{1,0:T(8,128)S(1)}, f32[4096,128]{1,0:T(8,128)}, u32[]{:S(2)}) copy-start(f32[4096,128]{1,0:T(8,128)} %fusion.63) | copy-start | bytes 6291460
  40.7 1.2 copy-start.2
  41.2 2.3 %copy-start.3 = (s32[1,32]{1,0:T(1,128)S(1)}, s32[1,32]{1,0:T(1,128)}, u32[]{:S(2)}) copy-start(s32[1,32]{1,0:T(1,128)} %param.5) | copy-start | bytes 388
  42.0 9.4 %collective-permute-start.1 = (bf16[2,256,256]{2,1,0:T(8,128)(2,1)S(1)}, bf16[2,256,256]{2,1,0:T(8,128)(2,1)S(1)}, u32[]{:S(2)}, u32[]{:S(2)}) collective-permute-start(bf16[2,256,256]{2,1,0:T(8,128)(2,1)S(1)} %slice.56), channel_id=1, source_target_pairs={{8,0},{16,8},{24,16},{9,1},{17,9},{25,17},{10,2},{18,10},{26,18},{... | collective-permute-start | bytes 786440 | tf_op jit(solution)/shard_map/ppermute | solution.py:17
  123.8 9.2 %copy-start.4 = (s32[1,1,8]{2,1,0:T(1,128)S(1)}, s32[1,1,8]{2,1,0:T(1,128)}, u32[]{:S(2)}) copy-start(s32[1,1,8]{2,1,0:T(1,128)} %param.4) | copy-start | bytes 100
Sparse Core Ops, SparseCore 0:
  133.1 27.9 all-gather.1
where the time goes:
time: 182 us; the launch traced here: 181 us
  local copies, waits for them, and re-layouts  97.6 us (54%)
  waiting for transfers between devices  42.7 us (23%)
  matrix products  21.3 us (12%)
  between operations  13.6 us (7%)
  other arithmetic  3.22 us (2%)
  starting transfers between devices  2.77 us (2%)
    reshape x1, local copies, waits for them, and re-layouts, cut_windows(): extended.reshape(2, pulses // per_block, per_block, span_bins)  60.6 us
    all_gather x1, waiting for transfers between devices, local(): all_blocks = lax.all_gather(windows, 'tile', axis=0, tiled=True)  27.7 us
    gather x2, local copies, waits for them, and re-layouts, one_block(): return lax.dynamic_slice_in_dim(block_data, start, WIN, 2)  20.7 us
    ppermute x2, waiting for transfers between devices, passed_along(): return lax.ppermute(value, axis, pairs)  15 us
    dot_general x1, matrix products, tile_image(): jnp.dot(interp, focused, preferred_element_type=jnp.float32)  7.65 us
    slice x1, local copies, waits for them, and re-layouts, compress(): real_in = paired[0]  4.49 us
    dot_general x1, matrix products, compress(): jnp.dot(real_in, real_tab, preferred_element_type=jnp.float32)  4.25 us
  transfers between devices with their start and end apart: 3, of which 3 were waited for; matrix products, arithmetic and copies ran while one was open for 0% of the time, Pallas kernels for 0%

commit v1 on v0

--- a/solution.py
+++ b/solution.py
@@ -109,7 +109,25 @@
     my_list = footprint[0, 0]
     tile_pos = lax.axis_index("tile")
     row_pos = lax.axis_index("section")
-    all_blocks = lax.all_gather(windows, "tile", axis=0, tiled=True)
+    count, index, rows = (lax.axis_size("tile"), lax.axis_index("tile"), windows.shape[0])
+    right = [(i_2, (i_2 + 1) % count) for i_2 in range(count)]
+    left = [(i_2, (i_2 - 1) % count) for i_2 in range(count)]
+    all_blocks = jnp.zeros(
+        (*windows.shape[:0], count * rows, *windows.shape[0 + 1 :]), windows.dtype
+    )
+    all_blocks = lax.dynamic_update_slice_in_dim(all_blocks, windows, index * rows, axis=0)
+    from_left = from_right = windows
+    middle = count // 2
+    for step in range(1, middle + 1):
+        from_left = lax.ppermute(from_left, "tile", right)
+        all_blocks = lax.dynamic_update_slice_in_dim(
+            all_blocks, from_left, (index - step) % count * rows, axis=0
+        )
+        if step < count - middle:
+            from_right = lax.ppermute(from_right, "tile", left)
+            all_blocks = lax.dynamic_update_slice_in_dim(
+                all_blocks, from_right, (index + step) % count * rows, axis=0
+            )
     chosen = jnp.take(all_blocks, my_list, axis=0)
     interp = interp_table(PR, WIN)
     image = tile_image(chosen, my_list, row_pos, tile_pos, interp, PC)

time: 182 us -> 169 us (0.929)
  between operations: 13.6 us -> 0.42 us
  starting transfers between devices: 2.77 us -> 10.5 us
  waiting for transfers between devices: 42.7 us -> 38.2 us
  local copies, waits for them, and re-layouts: 97.6 us -> 95.3 us
    all_gather x1 -> x0, waiting for transfers between devices: 27.7 us -> none  [local(): all_blocks = lax.all_gather(windows, 'tile', axis=0, tiled=True)]
    ppermute x0 -> x7, waiting for transfers between devices: none -> 23.1 us  [the longest x4 23.1 us: local(): from_left = lax.ppermute(from_left, 'tile', right)]
    ppermute x0 -> x7, starting transfers between devices: none -> 7.95 us  [the longest x3 7.88 us: local(): from_right = lax.ppermute(from_right, 'tile', left)]
  transfers between devices with their start and end apart: 3 -> 9, of which waited for: 3 -> 6; matrix products, arithmetic and copies ran while one was open for 0% -> 0% of each run, Pallas kernels for 0% -> 0%
where the time goes in v1:
time: 169 us
  local copies, waits for them, and re-layouts  95.3 us (56%)
  waiting for transfers between devices  38.2 us (23%)
  matrix products  21.2 us (13%)
  starting transfers between devices  10.5 us (6%)
  other arithmetic  3.23 us (2%)
    reshape x1, local copies, waits for them, and re-layouts, cut_windows(): extended.reshape(2, pulses // per_block, per_block, span_bins)  60.7 us
    ppermute x4, waiting for transfers between devices, local(): from_left = lax.ppermute(from_left, 'tile', right)  23.1 us
    gather x2, local copies, waits for them, and re-layouts, one_block(): return lax.dynamic_slice_in_dim(block_data, start, WIN, 2)  19.7 us
    ppermute x2, waiting for transfers between devices, passed_along(): return lax.ppermute(value, axis, pairs)  15.1 us
    ppermute x3, starting transfers between devices, local(): from_right = lax.ppermute(from_right, 'tile', left)  7.88 us
    dot_general x1, matrix products, tile_image(): jnp.dot(interp, focused, preferred_element_type=jnp.float32)  7.65 us
    slice x1, local copies, waits for them, and re-layouts, compress(): real_in = paired[0]  4.49 us
    dot_general x1, matrix products, compress(): jnp.dot(real_in, real_tab, preferred_element_type=jnp.float32)  4.26 us
  transfers between devices with their start and end apart: 9, of which 6 were waited for; matrix products, arithmetic and copies ran while one was open for 0% of the time, Pallas kernels for 0%

profile of v1, /device:TPU:0, one launch (start us, length us, event | category | flops | bytes accessed | tf_op | source)
XLA Modules:
  0.0 168.9 jit_solution(7943359819171000134)
XLA Ops:
  0.0 2.9 %copy.21 = bf16[2,256,2048]{1,2,0:T(8,128)(2,1)S(1)} copy(bf16[2,256,2048]{2,1,0:T(8,128)(2,1)} %param.3) | data formatting | bytes 4194304 | tf_op args[0]
  2.9 1.3 collective-permute-start
  4.2 7.1 %collective-permute-done = bf16[2,256,128]{1,2,0:T(8,128)(2,1)S(1)} collective-permute-done((bf16[2,256,128]{1,2,0:T(8,128)(2,1)S(1)}, bf16[2,256,128]{1,2,0:T(8,128)(2,1)S(1)}, u32[]{:S(2)}, u32[]{:S(2)}) %collective-permute-start) | collective-permute-done | bytes 131104 | tf_op jit(solution)/shard_map/ppermute | solution.py:17
  11.5 0.5 fusion.123
  12.0 2.3 %pad_maximum_fusion.1 = (bf16[1,256,16,256]{1,3,2,0:T(8,128)(2,1)}, bf16[1,256,16,256]{1,3,2,0:T(8,128)(2,1)}) fusion(bf16[2,256,16,128]{1,3,2,0:T(8,128)(2,1)S(1)} %get-tuple-element.9, bf16[2,256,16,128]{1,3,2,0:T(8,128)(2,1)S(1)} %get-tuple-element.10), kind=kLoop, calls=%fused_computation.12 | loop fusion | flops 8388608 | bytes 8388608 | tf_op jit(solution)/shard_map/concatenate | solution.py:39
  14.2 3.3 %copy.23 = bf16[1,256,16,256]{3,2,1,0:T(8,128)(2,1)S(1)} copy(bf16[1,256,16,256]{1,3,2,0:T(8,128)(2,1)} %get-tuple-element.7) | data formatting | bytes 4194304 | tf_op jit(solution)/shard_map/slice | solution.py:43
  17.6 2.5 %fusion.63 = f32[4096,128]{1,0:T(8,128)} fusion(bf16[4096,256]{1,0:T(8,128)(2,1)S(1)} %bitcast.27), kind=kOutput, calls=%fused_computation.95 | convolution fusion | flops 269156352 | bytes 4194304 | tf_op jit(solution)/shard_map/dot_general | solution.py:47
  20.1 4.5 %copy.22 = bf16[1,256,16,256]{3,2,1,0:T(8,128)(2,1)} copy(bf16[1,256,16,256]{1,3,2,0:T(8,128)(2,1)} %get-tuple-element.8) | data formatting | bytes 4194304 | tf_op jit(solution)/shard_map/slice | solution.py:42
  24.6 4.3 %fusion.64 = f32[4096,128]{1,0:T(8,128)} fusion(bf16[4096,256]{1,0:T(8,128)(2,1)} %bitcast.29), kind=kOutput, calls=%fused_computation.96 | convolution fusion | flops 269156352 | bytes 4194304 | tf_op jit(solution)/shard_map/dot_general | solution.py:44
  28.9 1.2 fusion.1
  30.1 1.3 stack.10
  31.4 2.8 %fusion = bf16[4096,128]{1,0:T(8,128)(2,1)S(1)} fusion(f32[4096,128]{1,0:T(8,128)} %fusion.64, bf16[4096,256]{1,0:T(8,128)(2,1)S(1)} %bitcast.28), kind=kOutput, calls=%fused_computation.4 | convolution fusion | flops 270204928 | bytes 5242880 | tf_op jit(solution)/shard_map/dot_general | solution.py:44
  34.2 0.5 stack.9
  34.8 0.6 copy-done.2
  35.5 1.3 collective-permute-start.1
  36.9 8.0 %collective-permute-done.1 = bf16[2,256,256]{2,1,0:T(8,128)(2,1)S(1)} collective-permute-done((bf16[2,256,256]{2,1,0:T(8,128)(2,1)S(1)}, bf16[2,256,256]{2,1,0:T(8,128)(2,1)S(1)}, u32[]{:S(2)}, u32[]{:S(2)}) %collective-permute-start.1) | collective-permute-done | bytes 262176 | tf_op jit(solution)/shard_map/ppermute | solution.py:17
  44.9 0.2 maximum_bitcast_fusion
  45.1 60.7 %copy.24 = bf16[2,32,8,2304]{2,0,1,3:T(2,128)(2,1)} copy(bf16[2,32,8,2304]{3,2,1,0:T(8,128)(2,1)S(1)} %maximum_bitcast_fusion) | data formatting | bytes 4718592 | tf_op jit(solution)/shard_map/reshape | solution.py:93
  105.8 11.5 %gather_fusion.1 = bf16[32,8,2,256]{1,2,3,0:T(2,128)(2,1)} fusion(bf16[32,8,2,2304]{1,2,0,3:T(2,128)(2,1)} %bitcast.26, s32[32]{0:T(128)S(1)} %fusion.78), kind=kCustom, calls=%fused_computation.1 | custom fusion | bytes 524800 | tf_op jit(solution)/shard_map/vmap()/gather | solution.py:97
  117.3 8.1 %copy.25 = bf16[32,8,2,256]{3,1,2,0:T(8,128)(2,1)S(1)} copy(bf16[32,8,2,256]{1,2,3,0:T(2,128)(2,1)} %gather_fusion.1) | data formatting | bytes 524288 | tf_op jit(solution)/shard_map/vmap()/gather | solution.py:97
  125.6 2.6 %collective-permute-start.3 = (bf16[32,8,2,256]{3,1,2,0:T(8,128)(2,1)S(1)}, bf16[32,8,2,256]{3,1,2,0:T(8,128)(2,1)S(1)}, u32[]{:S(2)}, u32[]{:S(2)}) collective-permute-start(bf16[32,8,2,256]{3,1,2,0:T(8,128)(2,1)S(1)} %copy.25), channel_id=1, source_target_pairs={{0,7},{1,0},{2,1},{3,2},{4,3},{5,4},{6,5},{7,6},{8,15},{9,8},{10,9... | collective-permute-start | bytes 786440 | tf_op jit(solution)/shard_map/ppermute | solution.py:127
  128.2 5.1 %collective-permute-done.2 = bf16[32,8,2,256]{3,1,2,0:T(8,128)(2,1)S(1)} collective-permute-done((bf16[32,8,2,256]{3,1,2,0:T(8,128)(2,1)S(1)}, bf16[32,8,2,256]{3,1,2,0:T(8,128)(2,1)S(1)}, u32[]{:S(2)}, u32[]{:S(2)}) %collective-permute-start.2) | collective-permute-done | bytes 262176 | tf_op jit(solution)/shard_map/ppermute | solution.py:122
  133.7 2.6 %collective-permute-start.5 = (bf16[32,8,2,256]{3,1,2,0:T(8,128)(2,1)S(1)}, bf16[32,8,2,256]{3,1,2,0:T(8,128)(2,1)S(1)}, u32[]{:S(2)}, u32[]{:S(2)}) collective-permute-start(bf16[32,8,2,256]{3,1,2,0:T(8,128)(2,1)S(1)} %collective-permute-done.3), channel_id=1, source_target_pairs={{0,7},{1,0},{2,1},{3,2},{4,3},{5,4},{6,5},{7,6},{8,15},{9,8},{10,9... | collective-permute-start | bytes 786440 | tf_op jit(solution)/shard_map/ppermute | solution.py:127
  136.4 5.2 %collective-permute-done.4 = bf16[32,8,2,256]{3,1,2,0:T(8,128)(2,1)S(1)} collective-permute-done((bf16[32,8,2,256]{3,1,2,0:T(8,128)(2,1)S(1)}, bf16[32,8,2,256]{3,1,2,0:T(8,128)(2,1)S(1)}, u32[]{:S(2)}, u32[]{:S(2)}) %collective-permute-start.4) | collective-permute-done | bytes 262176 | tf_op jit(solution)/shard_map/ppermute | solution.py:122
  141.7 2.7 %collective-permute-start.7 = (bf16[32,8,2,256]{3,1,2,0:T(8,128)(2,1)S(1)}, bf16[32,8,2,256]{3,1,2,0:T(8,128)(2,1)S(1)}, u32[]{:S(2)}, u32[]{:S(2)}) collective-permute-start(bf16[32,8,2,256]{3,1,2,0:T(8,128)(2,1)S(1)} %collective-permute-done.5), channel_id=1, source_target_pairs={{0,7},{1,0},{2,1},{3,2},{4,3},{5,4},{6,5},{7,6},{8,15},{9,8},{10,9... | collective-permute-start | bytes 786440 | tf_op jit(solution)/shard_map/ppermute | solution.py:127
  144.4 6.2 %collective-permute-done.6 = bf16[32,8,2,256]{3,1,2,0:T(8,128)(2,1)S(1)} collective-permute-done((bf16[32,8,2,256]{3,1,2,0:T(8,128)(2,1)S(1)}, bf16[32,8,2,256]{3,1,2,0:T(8,128)(2,1)S(1)}, u32[]{:S(2)}, u32[]{:S(2)}) %collective-permute-start.6) | collective-permute-done | bytes 262176 | tf_op jit(solution)/shard_map/ppermute | solution.py:122
  150.8 6.6 %collective-permute-done.8 = bf16[32,8,2,256]{3,1,2,0:T(8,128)(2,1)S(1)} collective-permute-done((bf16[32,8,2,256]{3,1,2,0:T(8,128)(2,1)S(1)}, bf16[32,8,2,256]{3,1,2,0:T(8,128)(2,1)S(1)}, u32[]{:S(2)}, u32[]{:S(2)}) %collective-permute-start.8) | collective-permute-done | bytes 262176 | tf_op jit(solution)/shard_map/ppermute | solution.py:122
  157.4 0.6 gather_fusion
  157.9 1.4 fusion.48
  159.3 1.4 fusion.49
  160.8 0.5 fusion.14
  161.3 7.6 %convert_bitcast_fusion = bf16[1,1,1024,2048]{3,2,1,0:T(8,128)(2,1)} fusion(bf16[256,1024]{1,0:T(8,128)(2,1)S(1)} %get-tuple-element.6, bf16[256,1024]{1,0:T(8,128)(2,1)S(1)} %get-tuple-element.5, f32[1024]{0:T(1024)S(1)} %multiply_add_fusion.1), kind=kOutput, calls=%fused_computation.8 | convolution fusion | flops 1088421888 | bytes 5246976 | tf_op jit(solution)/shard_map/dot_general | solution.py:86
  (41 shorter events, 1.1 us)
Async XLA Ops:
  0.0 4.2 %copy-start.4 = (s32[1,1,8]{2,1,0:T(1,128)S(1)}, s32[1,1,8]{2,1,0:T(1,128)}, u32[]{:S(2)}) copy-start(s32[1,1,8]{2,1,0:T(1,128)} %param.4) | copy-start | bytes 100
  2.9 8.4 %collective-permute-start = (bf16[2,256,128]{1,2,0:T(8,128)(2,1)S(1)}, bf16[2,256,128]{1,2,0:T(8,128)(2,1)S(1)}, u32[]{:S(2)}, u32[]{:S(2)}) collective-permute-start(bf16[2,256,128]{1,2,0:T(8,128)(2,1)S(1)} %slice.51), channel_id=1, source_target_pairs={{8,0},{16,8},{24,16},{9,1},{17,9},{25,17},{10,2},{18,10},{26,18},{... | collective-permute-start | bytes 393224 | tf_op jit(solution)/shard_map/ppermute | solution.py:17
  24.6 4.3 %copy-start = (bf16[1,256,16,256]{3,2,1,0:T(8,128)(2,1)S(1)}, bf16[1,256,16,256]{3,2,1,0:T(8,128)(2,1)}, u32[]{:S(2)}) copy-start(bf16[1,256,16,256]{3,2,1,0:T(8,128)(2,1)} %copy.22) | copy-start | bytes 6291460
  24.6 4.3 %copy-start.1 = (f32[4096,128]{1,0:T(8,128)S(1)}, f32[4096,128]{1,0:T(8,128)}, u32[]{:S(2)}) copy-start(f32[4096,128]{1,0:T(8,128)} %fusion.63) | copy-start | bytes 6291460
  34.2 1.2 copy-start.2
  34.7 2.1 %copy-start.3 = (s32[1,32]{1,0:T(1,128)S(1)}, s32[1,32]{1,0:T(1,128)}, u32[]{:S(2)}) copy-start(s32[1,32]{1,0:T(1,128)} %param.5) | copy-start | bytes 388
  35.5 9.4 %collective-permute-start.1 = (bf16[2,256,256]{2,1,0:T(8,128)(2,1)S(1)}, bf16[2,256,256]{2,1,0:T(8,128)(2,1)S(1)}, u32[]{:S(2)}, u32[]{:S(2)}) collective-permute-start(bf16[2,256,256]{2,1,0:T(8,128)(2,1)S(1)} %slice.56), channel_id=1, source_target_pairs={{8,0},{16,8},{24,16},{9,1},{17,9},{25,17},{10,2},{18,10},{26,18},{... | collective-permute-start | bytes 786440 | tf_op jit(solution)/shard_map/ppermute | solution.py:17
  125.5 7.8 %collective-permute-start.2 = (bf16[32,8,2,256]{3,1,2,0:T(8,128)(2,1)S(1)}, bf16[32,8,2,256]{3,1,2,0:T(8,128)(2,1)S(1)}, u32[]{:S(2)}, u32[]{:S(2)}) collective-permute-start(bf16[32,8,2,256]{3,1,2,0:T(8,128)(2,1)S(1)} %copy.25), channel_id=1, source_target_pairs={{0,1},{1,2},{2,3},{3,4},{4,5},{5,6},{6,7},{7,0},{8,9},{9,10},{10,1... | collective-permute-start | bytes 786440 | tf_op jit(solution)/shard_map/ppermute | solution.py:122
  125.6 8.1 %collective-permute-start.3 = (bf16[32,8,2,256]{3,1,2,0:T(8,128)(2,1)S(1)}, bf16[32,8,2,256]{3,1,2,0:T(8,128)(2,1)S(1)}, u32[]{:S(2)}, u32[]{:S(2)}) collective-permute-start(bf16[32,8,2,256]{3,1,2,0:T(8,128)(2,1)S(1)} %copy.25), channel_id=1, source_target_pairs={{0,7},{1,0},{2,1},{3,2},{4,3},{5,4},{6,5},{7,6},{8,15},{9,8},{10,9... | collective-permute-start | bytes 786440 | tf_op jit(solution)/shard_map/ppermute | solution.py:127
  133.3 8.4 %collective-permute-start.4 = (bf16[32,8,2,256]{3,1,2,0:T(8,128)(2,1)S(1)}, bf16[32,8,2,256]{3,1,2,0:T(8,128)(2,1)S(1)}, u32[]{:S(2)}, u32[]{:S(2)}) collective-permute-start(bf16[32,8,2,256]{3,1,2,0:T(8,128)(2,1)S(1)} %collective-permute-done.2), channel_id=1, source_target_pairs={{0,1},{1,2},{2,3},{3,4},{4,5},{5,6},{6,7},{7,0},{8,9},{9,10},{10,1... | collective-permute-start | bytes 786440 | tf_op jit(solution)/shard_map/ppermute | solution.py:122
  133.7 8.0 %collective-permute-start.5 = (bf16[32,8,2,256]{3,1,2,0:T(8,128)(2,1)S(1)}, bf16[32,8,2,256]{3,1,2,0:T(8,128)(2,1)S(1)}, u32[]{:S(2)}, u32[]{:S(2)}) collective-permute-start(bf16[32,8,2,256]{3,1,2,0:T(8,128)(2,1)S(1)} %collective-permute-done.3), channel_id=1, source_target_pairs={{0,7},{1,0},{2,1},{3,2},{4,3},{5,4},{6,5},{7,6},{8,15},{9,8},{10,9... | collective-permute-start | bytes 786440 | tf_op jit(solution)/shard_map/ppermute | solution.py:127
  141.6 9.0 %collective-permute-start.6 = (bf16[32,8,2,256]{3,1,2,0:T(8,128)(2,1)S(1)}, bf16[32,8,2,256]{3,1,2,0:T(8,128)(2,1)S(1)}, u32[]{:S(2)}, u32[]{:S(2)}) collective-permute-start(bf16[32,8,2,256]{3,1,2,0:T(8,128)(2,1)S(1)} %collective-permute-done.4), channel_id=1, source_target_pairs={{0,1},{1,2},{2,3},{3,4},{4,5},{5,6},{6,7},{7,0},{8,9},{9,10},{10,1... | collective-permute-start | bytes 786440 | tf_op jit(solution)/shard_map/ppermute | solution.py:122
  141.7 9.0 %collective-permute-start.7 = (bf16[32,8,2,256]{3,1,2,0:T(8,128)(2,1)S(1)}, bf16[32,8,2,256]{3,1,2,0:T(8,128)(2,1)S(1)}, u32[]{:S(2)}, u32[]{:S(2)}) collective-permute-start(bf16[32,8,2,256]{3,1,2,0:T(8,128)(2,1)S(1)} %collective-permute-done.5), channel_id=1, source_target_pairs={{0,7},{1,0},{2,1},{3,2},{4,3},{5,4},{6,5},{7,6},{8,15},{9,8},{10,9... | collective-permute-start | bytes 786440 | tf_op jit(solution)/shard_map/ppermute | solution.py:127
  150.7 6.7 %collective-permute-start.8 = (bf16[32,8,2,256]{3,1,2,0:T(8,128)(2,1)S(1)}, bf16[32,8,2,256]{3,1,2,0:T(8,128)(2,1)S(1)}, u32[]{:S(2)}, u32[]{:S(2)}) collective-permute-start(bf16[32,8,2,256]{3,1,2,0:T(8,128)(2,1)S(1)} %collective-permute-done.6), channel_id=1, source_target_pairs={{0,1},{1,2},{2,3},{3,4},{4,5},{5,6},{6,7},{7,0},{8,9},{9,10},{10,1... | collective-permute-start | bytes 786440 | tf_op jit(solution)/shard_map/ppermute | solution.py:122
